TPU v7x, 32 devices: a whole 2x2x4 slice. The times are simulated.
32 devices in a mesh: row: 4 (over z), col: 8 (over y, x, core).
Axes of the slice: x: 2, y: 2, z: 4, core: 2. Of those that a mesh axis runs over, the one named last changes fastest.
Arguments:
- unfolding: bfloat16 [3072, 4096], P('row', 'col'), may hold values from -400 to 400
Outputs:
- regrouped: bfloat16 [256, 16, 3072], P('col', None, 'row')
All inputs are finite; a program needn't handle non-finite values.
Results may differ from a plain program's by a relative error of at most 0.0062.
Values may be sent and summed in bfloat16 or wider, within the bound.
A program may use at most 64 MiB of HBM per device.

v0:
```python
import functools
import math

import jax
import jax.numpy as jnp
from jax import lax
from jax.experimental import pallas as pl
from jax.experimental.pallas import tpu as pltpu
from jax.sharding import PartitionSpec as P

PIXELS = 256
ITERS = 2
COLS = 4096
MESH = pl.DeviceIdType.MESH


def exchange(nr, nc, x_ref, out_ref, h_ref, xg, part, sendb, recvb, ssg, full, floats, halves, turned,
             own_sem, a_s, a_r, b_s, b_r, d_s, d_r, s_s, s_r, f_s, f_r, g_s, g_r, o_s, o_r):
    r = lax.axis_index("row")
    c = lax.axis_index("col")
    rd = x_ref.shape[0]
    w = x_ref.shape[1] // nr
    st = part.shape[0]
    ch = st // nr

    barrier = pltpu.get_barrier_semaphore()
    for k in range(nr):
        for m in range(nc):
            if k or m:
                pl.semaphore_signal(
                    barrier, inc=1, device_id=(lax.rem(r + k, nr), lax.rem(c + m, nc)), device_id_type=MESH)
    pl.semaphore_wait(barrier, nr * nc - 1)

    def lanes(index):
        return pl.ds(pl.multiple_of(index * w, w), w)

    def rows(index, size):
        return pl.ds(pl.multiple_of(index * size, size), size)

    def to_row(src, dst, s_sem, r_sem, k):
        return pltpu.make_async_remote_copy(
            src_ref=src, dst_ref=dst, send_sem=s_sem, recv_sem=r_sem,
            device_id=(lax.rem(r + k, nr), c), device_id_type=MESH)

    def to_col(src, dst, s_sem, r_sem, d):
        return pltpu.make_async_remote_copy(
            src_ref=src, dst_ref=dst, send_sem=s_sem, recv_sem=r_sem,
            device_id=(r, c ^ d), device_id_type=MESH)

    def gather_col(view, s_sem, r_sem, ready, landed):
        copies = {}

        def send(k, piece, slot, d, part=None):
            ref = view(k, piece)
            if part is not None:
                size = ref.shape[0] // 2
                ref = ref.at[pl.ds(part * size, size), :]
            copies[k, slot] = to_col(ref, ref, s_sem.at[k, slot], r_sem.at[k, slot], d)
            copies[k, slot].start()

        def relay(k):
            copies[k, 2].wait_recv()
            send(k, c ^ 2, 6, 4, 0)
            send(k, c ^ 2, 3, 1)
            copies[k, 4].wait_recv()
            send(k, c ^ 4, 0, 2, 1)
            send(k, c ^ 4, 5, 1)

        def relay_far(k):
            copies[k, 6].wait_recv()
            copies[k, 0].wait_recv()
            send(k, c ^ 6, 7, 1)

        for k in range(nr):
            ready(k)
            for d in (2, 4, 1):
                send(k, c, d, d)
            if k:
                relay(k - 1)
            if k > 1:
                relay_far(k - 2)
        relay(nr - 1)
        for k in range(max(nr - 2, 0), nr):
            relay_far(k)
        for d in (0, 2, 4, 6, 1, 3, 5, 7):
            if d % 2:
                for k in range(nr):
                    copies[k, d].wait_recv()
            landed(c ^ d)
        for key in copies:
            copies[key].wait_send()

    a = {}
    for k in range(1, nr):
        a[k] = to_row(x_ref.at[:, lanes(lax.rem(r + k, nr))], xg.at[rows(r, rd), lanes(c)],
                      a_s.at[k], a_r.at[k], k)
        a[k].start()
    own = pltpu.make_async_copy(x_ref.at[:, lanes(r)], xg.at[rows(r, rd), lanes(c)], own_sem)
    own.start()

    def ready_x(k):
        if k == 0:
            own.wait()
        else:
            a[k].wait_recv()

    gather_col(lambda k, piece: xg.at[rows(lax.rem(r + nr - k, nr), rd), lanes(piece)],
               b_s, b_r, ready_x, lambda piece: None)
    for k in range(1, nr):
        a[k].wait_send()

    left = xg[rows(c, st), :]
    for j in range(nc // 2 + 1):
        right = xg[rows(lax.rem(c + j, nc), st), :]
        block = lax.dot_general(left, right, (((1,), (1,)), ((), ())), preferred_element_type=jnp.float32)
        part[:, j * st:(j + 1) * st] = block
        sendb[:, j * st:(j + 1) * st] = block.astype(jnp.bfloat16)

    dc = {}
    for k in range(1, nr):
        dc[k] = to_row(sendb.at[rows(lax.rem(r + k, nr), ch), :], recvb.at[k - 1], d_s.at[k], d_r.at[k], k)
        dc[k].start()

    step = 32

    def body(i, acc):
        v = xg[rows(i, step), :].astype(jnp.float32)
        v = v * v
        t = acc
        for m in range(step // 8):
            for n in range(v.shape[1] // 128):
                t = t + v[8 * m:8 * m + 8, 128 * n:128 * n + 128]
        return t

    ssg[0] = lax.fori_loop(0, xg.shape[0] // step, body, jnp.zeros((8, 128), jnp.float32))
    sc = {}
    for k in range(1, nr):
        sc[k] = to_row(ssg.at[0], ssg.at[k], s_s.at[k], s_r.at[k], k)
        sc[k].start()
    for k in range(1, nr):
        dc[k].wait_recv()
    total = part[rows(r, ch), :]
    for k in range(1, nr):
        total = total + recvb[k - 1].astype(jnp.float32)
    h_ref[rows(c * nr + r, ch), :] = total.astype(jnp.bfloat16)

    fc = {}
    for k in range(1, nr):
        mine = h_ref.at[rows(c * nr + r, ch), :]
        fc[k] = to_row(mine, mine, f_s.at[k], f_r.at[k], k)
        fc[k].start()

    def ready_h(k):
        if k > 0:
            fc[k].wait_recv()

    half = nc // 2

    def mirror(i):
        def turn(index, carry):
            d, t = index // (st // 128), lax.rem(index, st // 128)
            j = lax.rem(i + d, nc)
            piece = h_ref[pl.ds(pl.multiple_of(i * st + t * 128, 128), 128), lanes_of(d * st, st)]
            full[rows(j, st), lanes_of(i * st + t * 128, 128)] = piece.T
            return carry

        def keep(d, carry):
            full[rows(i, st), lanes_of(lax.rem(i + d, nc) * st, st)] = h_ref[rows(i, st), lanes_of(d * st, st)]
            return carry

        lax.fori_loop(0, half + 1, keep, 0)
        lax.fori_loop(st // 128, half * (st // 128), turn, 0)

    def lanes_of(start, size):
        return pl.ds(pl.multiple_of(start, 128), size)

    gather_col(lambda k, piece: h_ref.at[rows(piece * nr + lax.rem(r + nr - k, nr), ch), :],
               g_s, g_r, ready_h, mirror)
    for k in range(1, nr):
        sc[k].wait_recv()
    tot = ssg[0]
    for k in range(1, nr):
        tot = tot + ssg[k]
    for k in range(1, nr):
        dc[k].wait_send()
        sc[k].wait_send()
        fc[k].wait_send()

    sumsq = jnp.full((8, 128), jnp.sum(tot), jnp.float32)
    factor = (math.sqrt(w * nr * nc) / (3.0 * jnp.sqrt(sumsq)))[0:1, :]
    square = factor * factor

    def product(src, emit):
        def tile(m, carry):
            at = rows(m, st)
            emit(at, square * jnp.dot(full[at, :], halves[src], preferred_element_type=jnp.float32))
            return carry

        lax.fori_loop(0, nc, tile, 0)

    def store(slot):
        def emit(at, value):
            floats[slot, at, :] = value
            halves[slot, at, :] = value.astype(jnp.bfloat16)
        return emit

    def poly(src, temp, dst):
        product(src, store(temp))
        product(temp, lambda at, two: store(dst)(
            at, 1.875 * floats[src, at, :] - 1.25 * floats[temp, at, :] + 0.375 * two))

    def begin(m, carry):
        store(0)(rows(m, st), factor * xg[rows(m, st), lanes(c)].astype(jnp.float32))
        return carry

    lax.fori_loop(0, nc, begin, 0)
    poly(0, 1, 2)

    def follow(m, carry):
        floats[4, rows(m, st), :] = 1.875 * floats[2, rows(m, st), :]
        return carry

    lax.fori_loop(0, nc, follow, 0)

    def level(turn_index, carry):
        weight = jnp.where(turn_index == 0, -1.25, 0.375)
        poly(2, 1, 0)
        poly(0, 1, 3)

        def emit(at, value):
            halves[2, at, :] = value.astype(jnp.bfloat16)
            floats[2, at, :] = value
            floats[4, at, :] += weight * value

        product(3, emit)
        return carry

    lax.fori_loop(0, 2, level, 0)

    scale = math.sqrt(xg.shape[0])

    def flip(m, carry):
        piece = (scale * floats[4, pl.ds(pl.multiple_of(m * 128, 128), 128), :]).T
        turned[m // (rd // 128), :, lanes_of(lax.rem(m, rd // 128) * 128, 128)] = piece.astype(jnp.bfloat16)
        return carry

    lax.fori_loop(0, nr * rd // 128, flip, 0)

    first_col = (c * nr + r) * w
    qd = PIXELS // nc
    share = w // qd
    view = first_col // PIXELS
    base = lax.rem(first_col, PIXELS) // qd
    copies = []
    for k in range(nr):
        for t in range(share):
            to = lax.rem(r + k, nr)
            src = turned.at[to, pl.ds(t * qd, qd), :]
            dst = out_ref.at[view]
            copy = pltpu.make_async_remote_copy(
                src_ref=src, dst_ref=dst, send_sem=o_s.at[k * share + t], recv_sem=o_r.at[view],
                device_id=(to, base + t), device_id_type=MESH)
            if k:
                copy.start()
                copies.append((None, copy))
            else:
                other = base + t != c

                @pl.when(other)
                def _(copy=copy):
                    copy.start()

                @pl.when(jnp.logical_not(other))
                def _(src=src, dst=dst):
                    mine = pltpu.make_async_copy(src, dst, own_sem)
                    mine.start()
                    mine.wait()

                copies.append((other, copy))
    for v in range(out_ref.shape[0]):
        source = (v * PIXELS + (c * qd // w) * w) // w
        away = source != c * nr + r

        @pl.when(away)
        def _(v=v):
            pltpu.make_async_remote_copy(
                src_ref=turned.at[0, pl.ds(0, qd), :], dst_ref=out_ref.at[v], send_sem=o_s.at[0],
                recv_sem=o_r.at[v], device_id=(lax.rem(r + 1, nr), c), device_id_type=MESH).wait_recv()
    for other, copy in copies:
        if other is None:
            copy.wait_send()
        else:
            pl.when(other)(lambda copy=copy: copy.wait_send())


def local_rows(unfolding, nr, nc):
    rd, cd = unfolding.shape
    total_rows = rd * nr
    w = cd // nr
    st = total_rows // nc
    half = (nc // 2 + 1) * st
    views = cd * nc // PIXELS
    vm = pl.BlockSpec(memory_space=pltpu.VMEM)
    dma = pltpu.SemaphoreType.DMA
    blocks = pl.pallas_call(
        functools.partial(exchange, nr, nc),
        out_shape=jax.ShapeDtypeStruct((views, PIXELS // nc, rd), jnp.bfloat16),
        in_specs=[vm],
        out_specs=vm,
        scratch_shapes=[
            pltpu.VMEM((total_rows, half), jnp.bfloat16),
            pltpu.VMEM((total_rows, nc * w), jnp.bfloat16),
            pltpu.VMEM((st, half), jnp.float32),
            pltpu.VMEM((st, half), jnp.bfloat16),
            pltpu.VMEM((nr - 1, st // nr, half), jnp.bfloat16),
            pltpu.VMEM((nr, 8, 128), jnp.float32),
            pltpu.VMEM((total_rows, total_rows), jnp.bfloat16),
            pltpu.VMEM((5, total_rows, w), jnp.float32),
            pltpu.VMEM((4, total_rows, w), jnp.bfloat16),
            pltpu.VMEM((nr, w, rd), jnp.bfloat16),
            dma, dma((nr,)), dma((nr,)), dma((nr, nc)), dma((nr, nc)),
            dma((nr,)), dma((nr,)), dma((nr,)), dma((nr,)),
            dma((nr,)), dma((nr,)), dma((nr, nc)), dma((nr, nc)),
            dma((nr * nc,)), dma((views,)),
        ],
        compiler_params=pltpu.CompilerParams(
            collective_id=0, has_side_effects=True, vmem_limit_bytes=63 * 1024 * 1024),
    )(unfolding)
    return blocks.transpose(1, 0, 2)


def local_cols(unfolding):
    rows_dev = unfolding.shape[0]
    cols_dev = unfolding.shape[1]
    total_rows = rows_dev * lax.axis_size("row")
    values = unfolding.astype(jnp.float32)
    sumsq = lax.psum(jnp.sum(values * values), ("row", "col"))
    factor = math.sqrt(COLS) / (3.0 * jnp.sqrt(sumsq))
    current = (values * factor).astype(jnp.bfloat16)
    updated = current.astype(jnp.float32)
    for turn_index in range(ITERS):
        gathered = lax.all_gather(current, "col", axis=1, tiled=True)
        partial_gram = lax.dot_general(
            current, gathered, (((0,), (0,)), ((), ())), preferred_element_type=jnp.float32
        )
        shares = lax.psum_scatter(partial_gram, "row", scatter_dimension=1, tiled=True).astype(
            jnp.bfloat16
        )
        gram_rows = lax.all_gather(shares, "row", axis=1, tiled=True)
        first = lax.dot_general(
            gathered, gram_rows, (((1,), (1,)), ((), ())), preferred_element_type=jnp.float32
        ).astype(jnp.bfloat16)
        second = lax.dot_general(
            lax.all_gather(first, "col", axis=1, tiled=True),
            gram_rows,
            (((1,), (1,)), ((), ())),
            preferred_element_type=jnp.float32,
        )
        updated = (
            1.875 * current.astype(jnp.float32) - 1.25 * first.astype(jnp.float32) + 0.375 * second
        )
        if turn_index + 1 < ITERS:
            current = updated.astype(jnp.bfloat16)
    final = updated * math.sqrt(total_rows)
    view_count = cols_dev // PIXELS
    cube = final.reshape(rows_dev, view_count, PIXELS).transpose(2, 1, 0).astype(jnp.bfloat16)
    return lax.all_to_all(cube, "col", split_axis=0, concat_axis=1, tiled=True)


def solution(mesh):
    nr, nc = mesh.shape["row"], mesh.shape["col"]

    def local(unfolding):
        rd, cd = unfolding.shape
        w = cd // nr
        fits = w == 128 and cd % (128 * nr) == 0 and nc == 8 and rd % 32 == 0 and (rd * nr) % (128 * nc) == 0 and (rd // nc) % 32 == 0
        fits = fits and PIXELS % w == 0 and w % (PIXELS // nc) == 0 and rd % 128 == 0 and ITERS == 2
        if rd * nr <= cd * nc and fits:
            return local_rows(unfolding, nr, nc)
        return local_cols(unfolding)

    return jax.shard_map(
        local,
        mesh=mesh,
        in_specs=(P("row", "col"),),
        out_specs=P("col", None, "row"),
        check_vma=False,
    )
```

profile of v0, /device:TPU:11, one launch (start us, length us, event | category | flops | bytes accessed | tf_op | source)
XLA Modules:
  0.0 247.0 jit_solution(16512787676855488778)
XLA Ops:
  0.0 244.6 %shard_map.17 = bf16[16,32,768]{2,1,0:T(8,128)(2,1)} custom-call(bf16[768,512]{1,0:T(8,128)(2,1)} %x_ref.1), custom_call_target="tpu_custom_call" | custom-call | tf_op jit(solution)/shard_map/pallas_call | solution.py:305
  244.6 2.4 copy.2
where the time goes:
time: 247 us
  Pallas kernels  245 us (99%)
    pallas_call x1, Pallas kernels, local_rows(): pl.pallas_call(functools.partial(exchange, nr, nc), out_shape=jax.ShapeDt...  245 us

commit v1 on v0

--- a/solution.py
+++ b/solution.py
@@ -14,8 +14,8 @@
 MESH = pl.DeviceIdType.MESH
 
 
-def exchange(nr, nc, x_ref, out_ref, h_ref, xg, part, sendb, recvb, ssg, full, floats, halves, turned,
-             own_sem, a_s, a_r, b_s, b_r, d_s, d_r, s_s, s_r, f_s, f_r, g_s, g_r, o_s, o_r):
+def exchange(nr, nc, x_ref, out_ref, h_ref, xg, part, sendb, recvb, ssg, full, floats, halves, acc, turned,
+             own_sem, a_s, a_r, b_s, b_r, d_s, d_r, s_s, s_r, f_s, f_r, g_s, g_r, x_s, x_r, o_s, o_r):
     r = lax.axis_index("row")
     c = lax.axis_index("col")
     rd = x_ref.shape[0]
@@ -155,20 +155,32 @@
             fc[k].wait_recv()
 
     half = nc // 2
+    core = lax.rem(c, 2)
+    first = c - core
+    hr = full.shape[0]
+    mine_from = core * half
 
     def mirror(i):
         def turn(index, carry):
             d, t = index // (st // 128), lax.rem(index, st // 128)
             j = lax.rem(i + d, nc)
-            piece = h_ref[pl.ds(pl.multiple_of(i * st + t * 128, 128), 128), lanes_of(d * st, st)]
-            full[rows(j, st), lanes_of(i * st + t * 128, 128)] = piece.T
+
+            @pl.when(j // half == core)
+            def _():
+                piece = h_ref[pl.ds(pl.multiple_of(i * st + t * 128, 128), 128), lanes_of(d * st, st)]
+                full[rows(j - mine_from, st), lanes_of(i * st + t * 128, 128)] = piece.T
+
             return carry
 
         def keep(d, carry):
-            full[rows(i, st), lanes_of(lax.rem(i + d, nc) * st, st)] = h_ref[rows(i, st), lanes_of(d * st, st)]
+            full[rows(i - mine_from, st), lanes_of(lax.rem(i + d, nc) * st, st)] = (
+                h_ref[rows(i, st), lanes_of(d * st, st)])
             return carry
 
-        lax.fori_loop(0, half + 1, keep, 0)
+        @pl.when(i // half == core)
+        def _():
+            lax.fori_loop(0, half + 1, keep, 0)
+
         lax.fori_loop(st // 128, half * (st // 128), turn, 0)
 
     def lanes_of(start, size):
@@ -186,85 +198,124 @@
         sc[k].wait_send()
         fc[k].wait_send()
 
-    sumsq = jnp.full((8, 128), jnp.sum(tot), jnp.float32)
+    sumsq = jnp.full((8, 2 * w), jnp.sum(tot), jnp.float32)
     factor = (math.sqrt(w * nr * nc) / (3.0 * jnp.sqrt(sumsq)))[0:1, :]
     square = factor * factor
 
-    def product(src, emit):
-        def tile(m, carry):
-            at = rows(m, st)
-            emit(at, square * jnp.dot(full[at, :], halves[src], preferred_element_type=jnp.float32))
-            return carry
-
-        lax.fori_loop(0, nc, tile, 0)
+    tm = hr // 2
+    mine = pl.ds(pl.multiple_of(core * hr, 128), hr)
+    theirs = pl.ds(pl.multiple_of((1 - core) * hr, 128), hr)
+
+    def swap(slot, m):
+        at = pl.ds(m * tm, tm)
+        return pltpu.make_async_remote_copy(
+            src_ref=halves.at[slot, 0, at, :], dst_ref=halves.at[slot, 1, at, :],
+            send_sem=x_s.at[slot, m], recv_sem=x_r.at[slot, m],
+            device_id=(r, c + 1 - 2 * core), device_id_type=MESH)
+
+    def product(slot, emit, number, more=None):
+        new = 1 - slot
+        for m in range(2):
+            at = pl.ds(m * tm, tm)
+            acc[at, :] = jnp.dot(full[at, mine], halves[slot, 0], preferred_element_type=jnp.float32)
+        for m in range(2):
+            if number > 1:
+                swap(slot, m).wait_recv()
+            if number > 2:
+                swap(new, m).wait_send()
+        for m in range(2):
+            at = pl.ds(m * tm, tm)
+            value = square * (acc[at, :] + jnp.dot(
+                full[at, theirs], halves[slot, 1], preferred_element_type=jnp.float32))
+            value = emit(at, value)
+            halves[new, 0, at, :] = value.astype(jnp.bfloat16)
+            if more is None:
+                swap(new, m).start()
+            else:
+                pl.when(more)(lambda m=m: swap(new, m).start())
 
     def store(slot):
         def emit(at, value):
             floats[slot, at, :] = value
-            halves[slot, at, :] = value.astype(jnp.bfloat16)
+            return value
         return emit
 
-    def poly(src, temp, dst):
-        product(src, store(temp))
-        product(temp, lambda at, two: store(dst)(
-            at, 1.875 * floats[src, at, :] - 1.25 * floats[temp, at, :] + 0.375 * two))
+    def combine(src, temp, dst):
+        def emit(at, two):
+            return store(dst)(at, 1.875 * floats[src, at, :] - 1.25 * floats[temp, at, :] + 0.375 * two)
+        return emit
+
+    pair = pl.ds(pl.multiple_of(first * w, 128), 2 * w)
+    step = tm // 8
 
     def begin(m, carry):
-        store(0)(rows(m, st), factor * xg[rows(m, st), lanes(c)].astype(jnp.float32))
+        at = pl.ds(pl.multiple_of(m * step, step), step)
+        value = factor * xg[pl.ds(pl.multiple_of(core * hr + m * step, step), step), pair].astype(jnp.float32)
+        floats[0, at, :] = value
+        halves[0, 0, at, :] = value.astype(jnp.bfloat16)
+        other = factor * xg[pl.ds(pl.multiple_of((1 - core) * hr + m * step, step), step), pair].astype(jnp.float32)
+        halves[0, 1, at, :] = other.astype(jnp.bfloat16)
         return carry
 
-    lax.fori_loop(0, nc, begin, 0)
-    poly(0, 1, 2)
+    lax.fori_loop(0, hr // step, begin, 0)
+    product(0, store(1), 1)
+    product(1, combine(0, 1, 2), 2)
 
     def follow(m, carry):
-        floats[4, rows(m, st), :] = 1.875 * floats[2, rows(m, st), :]
+        at = pl.ds(pl.multiple_of(m * step, step), step)
+        floats[4, at, :] = 1.875 * floats[2, at, :]
         return carry
 
-    lax.fori_loop(0, nc, follow, 0)
+    lax.fori_loop(0, hr // step, follow, 0)
 
     def level(turn_index, carry):
         weight = jnp.where(turn_index == 0, -1.25, 0.375)
-        poly(2, 1, 0)
-        poly(0, 1, 3)
+
+        def inner(k, carry):
+            product(turn_index, store(1), 3)
+            product(1 - turn_index, combine(2, 1, 2), 3)
+            return carry
+
+        lax.fori_loop(0, 2, inner, 0)
 
         def emit(at, value):
-            halves[2, at, :] = value.astype(jnp.bfloat16)
             floats[2, at, :] = value
             floats[4, at, :] += weight * value
-
-        product(3, emit)
+            return value
+
+        product(turn_index, emit, 3, turn_index == 0)
         return carry
 
     lax.fori_loop(0, 2, level, 0)
+    for m in range(2):
+        swap(1, m).wait_send()
 
     scale = math.sqrt(xg.shape[0])
+    planes = hr // rd
 
     def flip(m, carry):
         piece = (scale * floats[4, pl.ds(pl.multiple_of(m * 128, 128), 128), :]).T
         turned[m // (rd // 128), :, lanes_of(lax.rem(m, rd // 128) * 128, 128)] = piece.astype(jnp.bfloat16)
         return carry
 
-    lax.fori_loop(0, nr * rd // 128, flip, 0)
-
-    first_col = (c * nr + r) * w
+    lax.fori_loop(0, hr // 128, flip, 0)
+
     qd = PIXELS // nc
     share = w // qd
-    view = first_col // PIXELS
-    base = lax.rem(first_col, PIXELS) // qd
     copies = []
-    for k in range(nr):
-        for t in range(share):
-            to = lax.rem(r + k, nr)
-            src = turned.at[to, pl.ds(t * qd, qd), :]
-            dst = out_ref.at[view]
-            copy = pltpu.make_async_remote_copy(
-                src_ref=src, dst_ref=dst, send_sem=o_s.at[k * share + t], recv_sem=o_r.at[view],
-                device_id=(to, base + t), device_id_type=MESH)
-            if k:
-                copy.start()
-                copies.append((None, copy))
-            else:
-                other = base + t != c
+    for e in range(2):
+        first_col = ((first + e) * nr + r) * w
+        view = first_col // PIXELS
+        base = lax.rem(first_col, PIXELS) // qd
+        for k in range(planes):
+            for t in range(share):
+                to = core * planes + k
+                src = turned.at[k, pl.ds(e * w + t * qd, qd), :]
+                dst = out_ref.at[view]
+                copy = pltpu.make_async_remote_copy(
+                    src_ref=src, dst_ref=dst, send_sem=o_s.at[(e * planes + k) * share + t], recv_sem=o_r.at[view],
+                    device_id=(to, base + t), device_id_type=MESH)
+                other = jnp.logical_or(base + t != c, to != r)
 
                 @pl.when(other)
                 def _(copy=copy):
@@ -272,25 +323,23 @@
 
                 @pl.when(jnp.logical_not(other))
                 def _(src=src, dst=dst):
-                    mine = pltpu.make_async_copy(src, dst, own_sem)
-                    mine.start()
-                    mine.wait()
+                    kept = pltpu.make_async_copy(src, dst, own_sem)
+                    kept.start()
+                    kept.wait()
 
                 copies.append((other, copy))
     for v in range(out_ref.shape[0]):
-        source = (v * PIXELS + (c * qd // w) * w) // w
-        away = source != c * nr + r
-
-        @pl.when(away)
+        group = (v * PIXELS + (c * qd // w) * w) // w
+        column = group // nr
+        source = (column - lax.rem(column, 2) + r // planes) * nr + lax.rem(group, nr)
+
+        @pl.when(source != c * nr + r)
         def _(v=v):
             pltpu.make_async_remote_copy(
                 src_ref=turned.at[0, pl.ds(0, qd), :], dst_ref=out_ref.at[v], send_sem=o_s.at[0],
                 recv_sem=o_r.at[v], device_id=(lax.rem(r + 1, nr), c), device_id_type=MESH).wait_recv()
     for other, copy in copies:
-        if other is None:
-            copy.wait_send()
-        else:
-            pl.when(other)(lambda copy=copy: copy.wait_send())
+        pl.when(other)(lambda copy=copy: copy.wait_send())
 
 
 def local_rows(unfolding, nr, nc):
@@ -314,14 +363,15 @@
             pltpu.VMEM((st, half), jnp.bfloat16),
             pltpu.VMEM((nr - 1, st // nr, half), jnp.bfloat16),
             pltpu.VMEM((nr, 8, 128), jnp.float32),
-            pltpu.VMEM((total_rows, total_rows), jnp.bfloat16),
-            pltpu.VMEM((5, total_rows, w), jnp.float32),
-            pltpu.VMEM((4, total_rows, w), jnp.bfloat16),
-            pltpu.VMEM((nr, w, rd), jnp.bfloat16),
+            pltpu.VMEM((total_rows // 2, total_rows), jnp.bfloat16),
+            pltpu.VMEM((5, total_rows // 2, 2 * w), jnp.float32),
+            pltpu.VMEM((2, 2, total_rows // 2, 2 * w), jnp.bfloat16),
+            pltpu.VMEM((total_rows // 2, 2 * w), jnp.float32),
+            pltpu.VMEM((nr // 2, 2 * w, rd), jnp.bfloat16),
             dma, dma((nr,)), dma((nr,)), dma((nr, nc)), dma((nr, nc)),
             dma((nr,)), dma((nr,)), dma((nr,)), dma((nr,)),
             dma((nr,)), dma((nr,)), dma((nr, nc)), dma((nr, nc)),
-            dma((nr * nc,)), dma((views,)),
+            dma((2, 2)), dma((2, 2)), dma((nr * nc,)), dma((views,)),
         ],
         compiler_params=pltpu.CompilerParams(
             collective_id=0, has_side_effects=True, vmem_limit_bytes=63 * 1024 * 1024),
@@ -374,7 +424,7 @@
         rd, cd = unfolding.shape
         w = cd // nr
         fits = w == 128 and cd % (128 * nr) == 0 and nc == 8 and rd % 32 == 0 and (rd * nr) % (128 * nc) == 0 and (rd // nc) % 32 == 0
-        fits = fits and PIXELS % w == 0 and w % (PIXELS // nc) == 0 and rd % 128 == 0 and ITERS == 2
+        fits = fits and PIXELS % w == 0 and nr % 2 == 0 and w % (PIXELS // nc) == 0 and rd % 128 == 0 and ITERS == 2
         if rd * nr <= cd * nc and fits:
             return local_rows(unfolding, nr, nc)
         return local_cols(unfolding)

time: 247 us -> 221 us (0.89)
  Pallas kernels: 245 us -> 218 us
    pallas_call x1, Pallas kernels: 245 us -> 218 us  [local_rows(): pl.pallas_call(functools.partial(exchange, nr, nc), out_shape=jax.ShapeDt...]
where the time goes in v1:
time: 221 us; the launch traced here: 220 us
  Pallas kernels  218 us (99%)
  local copies, waits for them, and re-layouts  2.45 us (1%)
    pallas_call x1, Pallas kernels, local_rows(): pl.pallas_call(functools.partial(exchange, nr, nc), out_shape=jax.ShapeDt...  218 us

profile of v1, /device:TPU:11, one launch (start us, length us, event | category | flops | bytes accessed | tf_op | source)
XLA Modules:
  0.0 220.4 jit_solution(3731710891471580769)
XLA Ops:
  0.0 217.9 %shard_map.17 = bf16[16,32,768]{2,1,0:T(8,128)(2,1)} custom-call(bf16[768,512]{1,0:T(8,128)(2,1)} %x_ref.1), custom_call_target="tpu_custom_call" | custom-call | tf_op jit(solution)/shard_map/pallas_call | solution.py:354
  217.9 2.4 %copy.2 = bf16[32,16,768]{2,1,0:T(8,128)(2,1)} copy(bf16[32,16,768]{2,0,1:T(8,128)(2,1)} %bitcast.1) | data formatting | bytes 1572864 | tf_op jit(solution)/shard_map/transpose | solution.py:379

commit v2 on v1

--- a/solution.py
+++ b/solution.py
@@ -47,7 +47,21 @@
             src_ref=src, dst_ref=dst, send_sem=s_sem, recv_sem=r_sem,
             device_id=(r, c ^ d), device_id_type=MESH)
 
-    def gather_col(view, s_sem, r_sem, ready, landed):
+    def by_distance(k):
+        plane = None
+        for at in range(nr):
+            choice = sorted(range(nr), key=lambda p: (abs(p - at), p))[k]
+            plane = choice if plane is None else jnp.where(r == at, choice, plane)
+        return plane
+
+    order = [by_distance(k) for k in range(nr)]
+
+    def to_plane(src, dst, s_sem, r_sem, plane):
+        return pltpu.make_async_remote_copy(
+            src_ref=src, dst_ref=dst, send_sem=s_sem, recv_sem=r_sem,
+            device_id=(plane, c), device_id_type=MESH)
+
+    def gather_col(count, lag, view, s_sem, r_sem, ready, landed):
         copies = {}
 
         def send(k, piece, slot, d, part=None):
@@ -71,30 +85,35 @@
             copies[k, 0].wait_recv()
             send(k, c ^ 6, 7, 1)
 
-        for k in range(nr):
+        for k in range(count):
             ready(k)
             for d in (2, 4, 1):
                 send(k, c, d, d)
-            if k:
-                relay(k - 1)
-            if k > 1:
-                relay_far(k - 2)
-        relay(nr - 1)
-        for k in range(max(nr - 2, 0), nr):
+            if k >= lag:
+                relay(k - lag)
+            if k >= 2 * lag:
+                relay_far(k - 2 * lag)
+        for k in range(count - lag, count):
+            relay(k)
+        for k in range(count - 2 * lag, count):
             relay_far(k)
         for d in (0, 2, 4, 6, 1, 3, 5, 7):
             if d % 2:
-                for k in range(nr):
+                for k in range(count):
                     copies[k, d].wait_recv()
             landed(c ^ d)
         for key in copies:
             copies[key].wait_send()
 
-    a = {}
-    for k in range(1, nr):
-        a[k] = to_row(x_ref.at[:, lanes(lax.rem(r + k, nr))], xg.at[rows(r, rd), lanes(c)],
-                      a_s.at[k], a_r.at[k], k)
-        a[k].start()
+    ahead = [lax.rem(r + k, nr) for k in range(nr)]
+    behind = [lax.rem(r + nr - k, nr) for k in range(nr)]
+
+    def spread(k):
+        return to_plane(x_ref.at[:, lanes(ahead[k])], xg.at[rows(r, rd), lanes(c)],
+                        a_s.at[k], a_r.at[k], ahead[k])
+
+    for k in range(1, nr):
+        spread(k).start()
     own = pltpu.make_async_copy(x_ref.at[:, lanes(r)], xg.at[rows(r, rd), lanes(c)], own_sem)
     own.start()
 
@@ -102,24 +121,70 @@
         if k == 0:
             own.wait()
         else:
-            a[k].wait_recv()
-
-    gather_col(lambda k, piece: xg.at[rows(lax.rem(r + nr - k, nr), rd), lanes(piece)],
+            spread(k).wait_recv()
+
+    gather_col(nr, 1, lambda k, piece: xg.at[rows(behind[k], rd), lanes(piece)],
                b_s, b_r, ready_x, lambda piece: None)
     for k in range(1, nr):
-        a[k].wait_send()
-
-    left = xg[rows(c, st), :]
-    for j in range(nc // 2 + 1):
-        right = xg[rows(lax.rem(c + j, nc), st), :]
-        block = lax.dot_general(left, right, (((1,), (1,)), ((), ())), preferred_element_type=jnp.float32)
-        part[:, j * st:(j + 1) * st] = block
-        sendb[:, j * st:(j + 1) * st] = block.astype(jnp.bfloat16)
-
-    dc = {}
-    for k in range(1, nr):
-        dc[k] = to_row(sendb.at[rows(lax.rem(r + k, nr), ch), :], recvb.at[k - 1], d_s.at[k], d_r.at[k], k)
-        dc[k].start()
+        spread(k).wait_send()
+
+    groups = nc // 2 + 1
+
+    def columns(g):
+        return pl.ds(g * st, st)
+
+    def block(g):
+        left = xg[rows(c, st), :]
+        right = xg[rows(lax.rem(c + g, nc), st), :]
+        value = lax.dot_general(left, right, (((1,), (1,)), ((), ())), preferred_element_type=jnp.float32)
+        part[:, g * st:(g + 1) * st] = value
+        sendb[:, g * st:(g + 1) * st] = value.astype(jnp.bfloat16)
+
+    def scatter(g, k):
+        return to_plane(sendb.at[rows(ahead[k], ch), columns(g)], recvb.at[k - 1, :, columns(g)],
+                        d_s.at[k, g], d_r.at[k, g], ahead[k])
+
+    def issue(g):
+        if g < groups:
+            for k in range(1, nr):
+                scatter(g, k).start()
+
+    def hop(g, k, up):
+        mine = h_ref.at[rows(c * nr + order[k], ch), columns(g)]
+        return to_plane(mine, mine, f_s.at[0 if up else 1, k, g], f_r.at[order[k], g], r + 1 if up else r - 1)
+
+    def hops(g, k, act):
+        if k == 0:
+            pl.when(r < nr - 1)(lambda: act(hop(g, k, True)))
+            pl.when(r > 0)(lambda: act(hop(g, k, False)))
+        else:
+            pl.when(jnp.logical_and(order[k] < r, r < nr - 1))(lambda: act(hop(g, k, True)))
+            pl.when(jnp.logical_and(order[k] > r, r > 0))(lambda: act(hop(g, k, False)))
+
+    done = []
+
+    def ready_h(q):
+        while len(done) <= min(1 * q, q + 0, groups * nr - 1):
+            advance(*divmod(len(done), nr))
+            done.append(q)
+
+    def advance(g, k):
+        if k == 0:
+            total = part[rows(r, ch), g * st:(g + 1) * st]
+            for m in range(1, nr):
+                scatter(g, m).wait_recv()
+                total = total + recvb[m - 1, :, g * st:(g + 1) * st].astype(jnp.float32)
+            h_ref[rows(c * nr + r, ch), g * st:(g + 1) * st] = total.astype(jnp.bfloat16)
+        else:
+            hop(g, k, True).wait_recv()
+        hops(g, k, lambda copy: copy.start())
+        if k == 0:
+            issue(g + 2)
+
+    for g in range(groups):
+        block(g)
+        if g < 2:
+            issue(g)
 
     step = 32
 
@@ -137,22 +202,6 @@
     for k in range(1, nr):
         sc[k] = to_row(ssg.at[0], ssg.at[k], s_s.at[k], s_r.at[k], k)
         sc[k].start()
-    for k in range(1, nr):
-        dc[k].wait_recv()
-    total = part[rows(r, ch), :]
-    for k in range(1, nr):
-        total = total + recvb[k - 1].astype(jnp.float32)
-    h_ref[rows(c * nr + r, ch), :] = total.astype(jnp.bfloat16)
-
-    fc = {}
-    for k in range(1, nr):
-        mine = h_ref.at[rows(c * nr + r, ch), :]
-        fc[k] = to_row(mine, mine, f_s.at[k], f_r.at[k], k)
-        fc[k].start()
-
-    def ready_h(k):
-        if k > 0:
-            fc[k].wait_recv()
 
     half = nc // 2
     core = lax.rem(c, 2)
@@ -186,7 +235,7 @@
     def lanes_of(start, size):
         return pl.ds(pl.multiple_of(start, 128), size)
 
-    gather_col(lambda k, piece: h_ref.at[rows(piece * nr + lax.rem(r + nr - k, nr), ch), :],
+    gather_col(groups * nr, 2, lambda q, piece: h_ref.at[rows(piece * nr + order[q % nr], ch), columns(q // nr)],
                g_s, g_r, ready_h, mirror)
     for k in range(1, nr):
         sc[k].wait_recv()
@@ -194,9 +243,12 @@
     for k in range(1, nr):
         tot = tot + ssg[k]
     for k in range(1, nr):
-        dc[k].wait_send()
         sc[k].wait_send()
-        fc[k].wait_send()
+    for g in range(groups):
+        for k in range(nr):
+            if k:
+                scatter(g, k).wait_send()
+            hops(g, k, lambda copy: copy.wait_send())
 
     sumsq = jnp.full((8, 2 * w), jnp.sum(tot), jnp.float32)
     factor = (math.sqrt(w * nr * nc) / (3.0 * jnp.sqrt(sumsq)))[0:1, :]
@@ -347,7 +399,8 @@
     total_rows = rd * nr
     w = cd // nr
     st = total_rows // nc
-    half = (nc // 2 + 1) * st
+    groups = nc // 2 + 1
+    half = groups * st
     views = cd * nc // PIXELS
     vm = pl.BlockSpec(memory_space=pltpu.VMEM)
     dma = pltpu.SemaphoreType.DMA
@@ -369,8 +422,8 @@
             pltpu.VMEM((total_rows // 2, 2 * w), jnp.float32),
             pltpu.VMEM((nr // 2, 2 * w, rd), jnp.bfloat16),
             dma, dma((nr,)), dma((nr,)), dma((nr, nc)), dma((nr, nc)),
-            dma((nr,)), dma((nr,)), dma((nr,)), dma((nr,)),
-            dma((nr,)), dma((nr,)), dma((nr, nc)), dma((nr, nc)),
+            dma((nr, groups)), dma((nr, groups)), dma((nr,)), dma((nr,)),
+            dma((2, nr, groups)), dma((nr, groups)), dma((groups * nr, nc)), dma((groups * nr, nc)),
             dma((2, 2)), dma((2, 2)), dma((nr * nc,)), dma((views,)),
         ],
         compiler_params=pltpu.CompilerParams(

time: 221 us -> 203 us (0.919)
  Pallas kernels: 218 us -> 200 us
    pallas_call x1, Pallas kernels: 218 us -> 200 us  [local_rows(): pl.pallas_call(functools.partial(exchange, nr, nc), out_shape=jax.ShapeDt...]
where the time goes in v2:
time: 203 us
  Pallas kernels  200 us (99%)
  local copies, waits for them, and re-layouts  2.45 us (1%)
    pallas_call x1, Pallas kernels, local_rows(): pl.pallas_call(functools.partial(exchange, nr, nc), out_shape=jax.ShapeDt...  200 us

profile of v2, /device:TPU:11, one launch (start us, length us, event | category | flops | bytes accessed | tf_op | source)
XLA Modules:
  0.0 202.9 jit_solution(10642966581475783608)
XLA Ops:
  0.0 200.5 %shard_map.17 = bf16[16,32,768]{2,1,0:T(8,128)(2,1)} custom-call(bf16[768,512]{1,0:T(8,128)(2,1)} %x_ref.1), custom_call_target="tpu_custom_call" | custom-call | tf_op jit(solution)/shard_map/pallas_call | solution.py:407
  200.5 2.4 %copy.2 = bf16[32,16,768]{2,1,0:T(8,128)(2,1)} copy(bf16[32,16,768]{2,0,1:T(8,128)(2,1)} %bitcast.1) | data formatting | bytes 1572864 | tf_op jit(solution)/shard_map/transpose | solution.py:432

commit v3 on v2

--- a/solution.py
+++ b/solution.py
@@ -67,8 +67,8 @@
         def send(k, piece, slot, d, part=None):
             ref = view(k, piece)
             if part is not None:
-                size = ref.shape[0] // 2
-                ref = ref.at[pl.ds(part * size, size), :]
+                size = ref.shape[0] // 32 * 16
+                ref = ref.at[pl.ds(part * size, ref.shape[0] - size if part else size), :]
             copies[k, slot] = to_col(ref, ref, s_sem.at[k, slot], r_sem.at[k, slot], d)
             copies[k, slot].start()
 
@@ -133,15 +133,25 @@
     def columns(g):
         return pl.ds(g * st, st)
 
+    def height(g):
+        return ch if g < groups - 1 else ch // 2
+
+    def chunk(g, piece, plane):
+        return pl.ds(pl.multiple_of(piece * st + plane * height(g), 16), height(g))
+
     def block(g):
-        left = xg[rows(c, st), :]
-        right = xg[rows(lax.rem(c + g, nc), st), :]
+        if g < groups - 1:
+            left = xg[rows(c, st), :]
+            right = xg[rows(lax.rem(c + g, nc), st), :]
+        else:
+            left = xg[rows(lax.rem(c, nc // 2) * 2 + c // (nc // 2), st // 2), :]
+            right = xg[rows(lax.rem(c, nc // 2) + nc // 2, st), :]
         value = lax.dot_general(left, right, (((1,), (1,)), ((), ())), preferred_element_type=jnp.float32)
-        part[:, g * st:(g + 1) * st] = value
-        sendb[:, g * st:(g + 1) * st] = value.astype(jnp.bfloat16)
+        part[0:nr * height(g), g * st:(g + 1) * st] = value
+        sendb[0:nr * height(g), g * st:(g + 1) * st] = value.astype(jnp.bfloat16)
 
     def scatter(g, k):
-        return to_plane(sendb.at[rows(ahead[k], ch), columns(g)], recvb.at[k - 1, :, columns(g)],
+        return to_plane(sendb.at[rows(ahead[k], height(g)), columns(g)], recvb.at[k - 1, pl.ds(0, height(g)), columns(g)],
                         d_s.at[k, g], d_r.at[k, g], ahead[k])
 
     def issue(g):
@@ -150,7 +160,7 @@
                 scatter(g, k).start()
 
     def hop(g, k, up):
-        mine = h_ref.at[rows(c * nr + order[k], ch), columns(g)]
+        mine = h_ref.at[chunk(g, c, order[k]), columns(g)]
         return to_plane(mine, mine, f_s.at[0 if up else 1, k, g], f_r.at[order[k], g], r + 1 if up else r - 1)
 
     def hops(g, k, act):
@@ -161,20 +171,18 @@
             pl.when(jnp.logical_and(order[k] < r, r < nr - 1))(lambda: act(hop(g, k, True)))
             pl.when(jnp.logical_and(order[k] > r, r > 0))(lambda: act(hop(g, k, False)))
 
-    done = []
+    items = sorted(((g, k) for g in range(groups) for k in range(nr)), key=lambda i: (2 * i[0] + i[1], i[0]))
 
     def ready_h(q):
-        while len(done) <= min(1 * q, q + 0, groups * nr - 1):
-            advance(*divmod(len(done), nr))
-            done.append(q)
+        advance(*items[q])
 
     def advance(g, k):
         if k == 0:
-            total = part[rows(r, ch), g * st:(g + 1) * st]
+            total = part[rows(r, height(g)), g * st:(g + 1) * st]
             for m in range(1, nr):
                 scatter(g, m).wait_recv()
-                total = total + recvb[m - 1, :, g * st:(g + 1) * st].astype(jnp.float32)
-            h_ref[rows(c * nr + r, ch), g * st:(g + 1) * st] = total.astype(jnp.bfloat16)
+                total = total + recvb[m - 1, 0:height(g), g * st:(g + 1) * st].astype(jnp.float32)
+            h_ref[chunk(g, c, r), g * st:(g + 1) * st] = total.astype(jnp.bfloat16)
         else:
             hop(g, k, True).wait_recv()
         hops(g, k, lambda copy: copy.start())
@@ -228,15 +236,43 @@
 
         @pl.when(i // half == core)
         def _():
-            lax.fori_loop(0, half + 1, keep, 0)
+            lax.fori_loop(0, half, keep, 0)
 
         lax.fori_loop(st // 128, half * (st // 128), turn, 0)
 
     def lanes_of(start, size):
         return pl.ds(pl.multiple_of(start, 128), size)
 
-    gather_col(groups * nr, 2, lambda q, piece: h_ref.at[rows(piece * nr + order[q % nr], ch), columns(q // nr)],
+    gather_col(groups * nr, 2, lambda q, piece: h_ref.at[chunk(items[q][0], piece, order[items[q][1]]), columns(items[q][0])],
                g_s, g_r, ready_h, mirror)
+
+    def across(a, carry):
+        low, high, hs = a * st, (a + half) * st, st // 2
+        cols = pl.ds(half * st, st)
+
+        def take(start, size):
+            return h_ref[pl.ds(pl.multiple_of(start, 16), size), cols]
+
+        @pl.when(core == 0)
+        def _():
+            full[pl.ds(pl.multiple_of(low, 16), hs), lanes_of(high, st)] = take(low, hs)
+            full[pl.ds(pl.multiple_of(low + hs, 16), hs), lanes_of(high, st)] = take(high, hs)
+
+        @pl.when(core == 1)
+        def _():
+            for t in range(st // 128):
+                start, stop = t * 128, t * 128 + 128
+                if stop <= hs:
+                    piece = take(low + start, 128)
+                elif start >= hs:
+                    piece = take(high + start - hs, 128)
+                else:
+                    piece = jnp.concatenate([take(low + start, hs - start), take(high, stop - hs)], axis=0)
+                full[rows(a, st), lanes_of(low + start, 128)] = piece.T
+
+        return carry
+
+    lax.fori_loop(0, half, across, 0)
     for k in range(1, nr):
         sc[k].wait_recv()
     tot = ssg[0]

time: 203 us -> 192 us (0.946)
  Pallas kernels: 200 us -> 189 us
    pallas_call x1, Pallas kernels: 200 us -> 189 us  [local_rows(): pl.pallas_call(functools.partial(exchange, nr, nc), out_shape=jax.ShapeDt...]
where the time goes in v3:
time: 192 us
  Pallas kernels  189 us (98%)
  local copies, waits for them, and re-layouts  2.45 us (1%)
    pallas_call x1, Pallas kernels, local_rows(): pl.pallas_call(functools.partial(exchange, nr, nc), out_shape=jax.ShapeDt...  189 us

profile of v3, /device:TPU:11, one launch (start us, length us, event | category | flops | bytes accessed | tf_op | source)
XLA Modules:
  0.0 191.7 jit_solution(2675295123917510804)
XLA Ops:
  0.0 189.2 %shard_map.17 = bf16[16,32,768]{2,1,0:T(8,128)(2,1)} custom-call(bf16[768,512]{1,0:T(8,128)(2,1)} %x_ref.1), custom_call_target="tpu_custom_call" | custom-call | tf_op jit(solution)/shard_map/pallas_call | solution.py:443
  189.2 2.4 %copy.2 = bf16[32,16,768]{2,1,0:T(8,128)(2,1)} copy(bf16[32,16,768]{2,0,1:T(8,128)(2,1)} %bitcast.1) | data formatting | bytes 1572864 | tf_op jit(solution)/shard_map/transpose | solution.py:468
